TPU v7x, 32 devices: a whole 2x2x4 slice. The times are simulated.
32 devices in a mesh: energy: 8 (over y, x, core), space: 4 (over z).
Axes of the slice: x: 2, y: 2, z: 4, core: 2. Of those that a mesh axis runs over, the one named last changes fastest.
Arguments:
- screening: bfloat16 [8, 8, 3, 2, 128, 128], P('energy', 'space'), may hold values from -0.21875 to 0.21875
- polarization: bfloat16 [8, 8, 3, 2, 128, 128], P('energy', 'space'), may hold values from -6 to 6
- propagator: bfloat16 [8, 8, 3, 2, 128, 128], P('energy', 'space'), may hold values from -0.21875 to 0.21875
Outputs:
- dressed: bfloat16 [8, 8, 3, 2, 128, 128], P('energy', 'space')
All inputs are finite; a program needn't handle non-finite values.
Results may differ from a plain program's by a relative error of at most 0.015.
Values may be sent and summed in bfloat16 or wider, within the bound.
No kernel may reach another device: no remote copies, remote signals or barrier semaphores. Data moves between devices by JAX's collectives and lax.ppermute only.
A program may use at most 64 MiB of HBM per device.

v0:
```python
import math
import jax
import jax.numpy as jnp
from jax import lax
from jax.sharding import PartitionSpec as P


def with_halo(x, sides, width):
    for axis, dim in sides:
        peers, length = (lax.axis_size(axis), x.shape[dim])
        up = [(i, (i + 1) % peers) for i in range(peers - 1)]
        down = [(j, i) for i, j in up]
        last = lax.slice_in_dim(x, length - width, length, axis=dim)
        leading = lax.slice_in_dim(x, 0, width, axis=dim)
        before = lax.ppermute(last, axis, up)
        after = lax.ppermute(leading, axis, down)
        x = jnp.concatenate([before, x, after], axis=dim)
    return x


def clip_edges(banded, first_row, row_total):
    row_count = banded.shape[1]
    row_index = first_row + jnp.arange(row_count, dtype=jnp.int32)
    band_index = jnp.arange(3, dtype=jnp.int32)
    dropped = (band_index[None, :] == 0) & (row_index[:, None] == 0) | (
        band_index[None, :] == 2
    ) & (row_index[:, None] == row_total - 1)
    keep_mask = jnp.where(dropped, 0.0, 1.0).astype(banded.dtype)
    return banded * keep_mask[None, :, :, None, None, None]


def complex_product(first, second, adjoint):
    first_real = first[:, :, 0]
    first_imag = first[:, :, 1]
    second_real = second[:, :, 0]
    second_imag = second[:, :, 1]
    if adjoint:
        form = "erij,erkj->erik"
    else:
        form = "erij,erjk->erik"

    def product(lhs, rhs):
        return jnp.einsum(form, lhs, rhs, preferred_element_type=jnp.float32)

    if adjoint:
        real_part = product(first_real, second_real) + product(first_imag, second_imag)
        imag_part = product(first_imag, second_real) - product(first_real, second_imag)
    else:
        real_part = product(first_real, second_real) - product(first_imag, second_imag)
        imag_part = product(first_real, second_imag) + product(first_imag, second_real)
    return jnp.stack([real_part, imag_part], axis=2)


def pick_rows(banded, start, row_count, band):
    return lax.slice_in_dim(banded, start, start + row_count, axis=1)[:, :, band]


def sandwich(outside, between):
    row_count = outside.shape[1] - 2
    products = {}
    for offset in range(-2, 3):
        summed = None
        for inner in range(-1, 2):
            if abs(offset - inner) <= 1:
                term = complex_product(
                    pick_rows(outside, 1, row_count, inner + 1),
                    pick_rows(between, 1 + inner, row_count, offset - inner + 1),
                    False,
                )
                summed = term if summed is None else summed + term
        products[offset] = summed.astype(jnp.bfloat16)
    bands = []
    for target in range(-1, 2):
        summed = None
        for offset in range(target - 1, target + 2):
            term = complex_product(
                products[offset],
                pick_rows(outside, 1 + target, row_count, offset - target + 1),
                True,
            )
            summed = term if summed is None else summed + term
        bands.append(summed)
    return jnp.stack(bands, axis=2)


def split_table(table):
    upper = table.astype(jnp.bfloat16)
    lower = (table - upper.astype(jnp.float32)).astype(jnp.bfloat16)
    return (upper, lower)


def plain_dot(lhs, rhs):
    return jnp.dot(lhs, rhs, preferred_element_type=jnp.float32)


def table_times_data(table_pair, data):
    return plain_dot(table_pair[0], data) + plain_dot(table_pair[1], data)


def table_times_float(table_pair, values):
    value_upper, value_lower = split_table(values)
    return (
        plain_dot(table_pair[0], value_upper)
        + plain_dot(table_pair[0], value_lower)
        + plain_dot(table_pair[1], value_upper)
    )


def convolve(propa_owned, screen_owned, factor):
    energy_count = propa_owned.shape[0]
    owned_shape = propa_owned[:, :, :, 0].shape
    freq_index = jnp.arange(2 * energy_count, dtype=jnp.int32)
    time_index = jnp.arange(energy_count, dtype=jnp.int32)
    phase = freq_index[:, None] * time_index[None, :] % (2 * energy_count)
    angle = phase.astype(jnp.float32) * (math.pi / energy_count)
    cosine = jnp.cos(angle)
    sine = jnp.sin(angle)
    cos_fwd = split_table(cosine)
    sin_fwd = split_table(sine)
    cos_back = split_table(cosine.T)
    sin_back = split_table(sine.T)

    def forward(banded):
        real_part = banded[:, :, :, 0].reshape(energy_count, -1)
        imag_part = banded[:, :, :, 1].reshape(energy_count, -1)
        return (
            table_times_data(cos_fwd, real_part) + table_times_data(sin_fwd, imag_part),
            table_times_data(cos_fwd, imag_part) - table_times_data(sin_fwd, real_part),
        )

    propa_real, propa_imag = forward(propa_owned)
    screen_real, screen_imag = forward(screen_owned)
    spec_real = propa_real * screen_real - propa_imag * screen_imag
    spec_imag = propa_real * screen_imag + propa_imag * screen_real
    weight = factor / (2 * energy_count)
    out_real = (
        table_times_float(cos_back, spec_real) - table_times_float(sin_back, spec_imag)
    ) * weight
    out_imag = (
        table_times_float(cos_back, spec_imag) + table_times_float(sin_back, spec_real)
    ) * weight
    return jnp.stack([out_real.reshape(owned_shape), out_imag.reshape(owned_shape)], axis=3)


def local(screening, polarization, propagator):
    row_count = screening.shape[1]
    order = screening.shape[-1]
    first_row = lax.axis_index("space") * row_count
    row_total = lax.axis_size("space") * row_count
    screen_masked = clip_edges(screening, first_row, row_total)
    polar_masked = clip_edges(polarization, first_row, row_total)
    propa_masked = clip_edges(propagator, first_row, row_total)
    rimmed = with_halo(jnp.stack([screen_masked, polar_masked, propa_masked]), (("space", 2),), 1)
    screen_padded = rimmed[0]
    polar_padded = rimmed[1]
    propa_padded = rimmed[2]
    screened = sandwich(screen_padded, polar_padded).astype(jnp.bfloat16)
    screen_owned, propa_owned = (
        lax.all_to_all(screened, "energy", split_axis=4, concat_axis=0, tiled=True),
        lax.all_to_all(propa_masked, "energy", split_axis=4, concat_axis=0, tiled=True),
    )
    energy_count = screen_owned.shape[0]
    factor = (3.0 * order / energy_count) ** 0.5
    sigma_owned = convolve(propa_owned, screen_owned, factor).astype(jnp.bfloat16)
    sigma = lax.all_to_all(sigma_owned, "energy", split_axis=0, concat_axis=4, tiled=True)
    sigma_padded = with_halo(sigma, (("space", 1),), 1)
    return sandwich(propa_padded, sigma_padded).astype(jnp.bfloat16)


def solution(mesh):
    in_specs = (
        P("energy", "space", None, None, None, None),
        P("energy", "space", None, None, None, None),
        P("energy", "space", None, None, None, None),
    )
    out_specs = P("energy", "space", None, None, None, None)
    return jax.shard_map(local, mesh=mesh, in_specs=in_specs, out_specs=out_specs, check_vma=False)
```

profile of v0, /device:TPU:0, one launch (start us, length us, event | category | flops | bytes accessed | tf_op | source)
XLA Modules:
  0.0 100.8 jit_solution(13113473520460223739)
XLA Ops:
  0.1 1.4 %fusion.83 = (bf16[1,1,2,3,2,128,128]{6,5,2,4,3,1,0:T(8,128)(2,1)S(1)}, bf16[1,1,2,3,2,128,128]{6,5,2,4,3,1,0:T(8,128)(2,1)S(1)}, bf16[1,2,3,2,128,128]{5,4,1,3,2,0:T(8,128)(2,1)S(1)}) fusion(bf16[1,2,3,2,128,128]{5,4,3,2,1,0:T(8,128)(2,1)} %param.3, bf16[2,3]{0,1:T(4,128)(2,1)S(1)} %select_convert_fusion, bf16[1,2,3,2,128,128]{5,4,3,2,1,0:T(8,128)(2,1)} %param.4, ...), kind=kLoop, calls=%fused_computation.188 | loop fusion | flops 589824 | bytes 2359308 | tf_op jit(solution)/shard_map/stack | solution.py:153
  1.5 1.2 %copy.19 = bf16[1,2,3,2,128,128]{5,1,3,2,0,4:T(2,128)(2,1)} copy(bf16[1,2,3,2,128,128]{5,4,1,3,2,0:T(8,128)(2,1)S(1)} %get-tuple-element.59) | data formatting | bytes 786432 | tf_op jit(solution)/shard_map/mul | solution.py:29
  2.6 5.2 %all-to-all-start = ((bf16[1,2,3,2,128,128]{5,1,3,2,0,4:T(2,128)(2,1)}), bf16[1,2,3,2,128,128]{5,1,3,2,0,4:T(2,128)(2,1)S(1)}, u32[]{:S(2)}, u32[]{:S(2)}) async-start(bf16[1,2,3,2,128,128]{5,1,3,2,0,4:T(2,128)(2,1)} %copy.19), calls=%async_computation | async-start | bytes 786432 | tf_op jit(solution)/shard_map/all_to_all | solution.py:160
  8.0 1.2 %fusion.358 = (bf16[3,1,1,3,2,128,128]{6,5,2,4,3,1,0:T(8,128)(2,1)}, bf16[3,1,1,3,2,128,128]{6,5,2,4,3,1,0:T(8,128)(2,1)}) fusion(bf16[3,1,2,3,2,128,128]{6,5,2,4,3,1,0:T(8,128)(2,1)S(1)} %pad_maximum_fusion.1), kind=kLoop, calls=%fused_computation.593 | loop fusion | bytes 2359296 | tf_op jit(solution)/shard_map/slice | solution.py:13
  9.1 4.3 %collective-permute-start = (bf16[3,1,1,3,2,128,128]{6,5,2,4,3,1,0:T(8,128)(2,1)}, bf16[3,1,1,3,2,128,128]{6,5,2,4,3,1,0:T(8,128)(2,1)}, u32[]{:S(2)}, u32[]{:S(2)}) collective-permute-start(bf16[3,1,1,3,2,128,128]{6,5,2,4,3,1,0:T(8,128)(2,1)} %get-tuple-element.10), channel_id=1, source_target_pairs={{0,1},{1,2},{2,3},{4,5},{5,6},{6,7},{8,9},{9,10},{10,11},{12,13},{... | collective-permute-start | bytes 1769480 | tf_op jit(solution)/shard_map/ppermute | solution.py:15
  13.4 1.3 %collective-permute-start.1 = (bf16[3,1,1,3,2,128,128]{6,5,2,4,3,1,0:T(8,128)(2,1)}, bf16[3,1,1,3,2,128,128]{6,5,2,4,3,1,0:T(8,128)(2,1)}, u32[]{:S(2)}, u32[]{:S(2)}) collective-permute-start(bf16[3,1,1,3,2,128,128]{6,5,2,4,3,1,0:T(8,128)(2,1)} %get-tuple-element.11), channel_id=1, source_target_pairs={{1,0},{2,1},{3,2},{5,4},{6,5},{7,6},{9,8},{10,9},{11,10},{13,12},{... | collective-permute-start | bytes 1769480 | tf_op jit(solution)/shard_map/ppermute | solution.py:16
  14.7 1.4 %all-to-all-done = bf16[1,2,3,2,128,128]{5,1,3,2,0,4:T(2,128)(2,1)S(1)} async-done(((bf16[1,2,3,2,128,128]{5,1,3,2,0,4:T(2,128)(2,1)}), bf16[1,2,3,2,128,128]{5,1,3,2,0,4:T(2,128)(2,1)S(1)}, u32[]{:S(2)}, u32[]{:S(2)}) %all-to-all-start) | async-done | bytes 393248 | tf_op jit(solution)/shard_map/all_to_all | solution.py:160
  16.3 1.2 %fusion.203 = f32[16,12288]{1,0:T(8,128)} fusion(bf16[8,12288]{1,0:T(8,128)(2,1)S(1)} %reshape_squeeze.13), kind=kOutput, calls=%fused_computation.447 | convolution fusion | flops 3147648 | bytes 983040 | tf_op jit(solution)/shard_map/dot_general | solution.py:93
  18.5 1.2 %convolution_add_fusion.3 = f32[16,12288]{1,0:T(8,128)} fusion(f32[16,12288]{1,0:T(8,128)S(1)} %fusion.207, bf16[8,12288]{1,0:T(8,128)(2,1)S(1)} %reshape_squeeze.13), kind=kOutput, calls=%fused_computation.5 | convolution fusion | flops 3344640 | bytes 1769472 | tf_op jit(solution)/shard_map/dot_general | solution.py:93
  19.7 6.4 %collective-permute-done = bf16[3,1,1,3,2,128,128]{6,5,2,4,3,1,0:T(8,128)(2,1)} collective-permute-done((bf16[3,1,1,3,2,128,128]{6,5,2,4,3,1,0:T(8,128)(2,1)}, bf16[3,1,1,3,2,128,128]{6,5,2,4,3,1,0:T(8,128)(2,1)}, u32[]{:S(2)}, u32[]{:S(2)}) %collective-permute-start) | collective-permute-done | bytes 589856 | tf_op jit(solution)/shard_map/ppermute | solution.py:15
  26.2 4.9 %collective-permute-done.1 = bf16[3,1,1,3,2,128,128]{6,5,2,4,3,1,0:T(8,128)(2,1)} collective-permute-done((bf16[3,1,1,3,2,128,128]{6,5,2,4,3,1,0:T(8,128)(2,1)}, bf16[3,1,1,3,2,128,128]{6,5,2,4,3,1,0:T(8,128)(2,1)}, u32[]{:S(2)}, u32[]{:S(2)}) %collective-permute-start.1) | collective-permute-done | bytes 589856 | tf_op jit(solution)/shard_map/ppermute | solution.py:16
  31.1 1.4 %pad_maximum_fusion = bf16[3,1,4,3,2,128,128]{6,5,2,4,3,1,0:T(8,128)(2,1)S(1)} fusion(bf16[3,1,1,3,2,128,128]{6,5,2,4,3,1,0:T(8,128)(2,1)} %collective-permute-done.1, bf16[1,1,2,3,2,128,128]{6,5,2,4,3,1,0:T(8,128)(2,1)S(1)} %bitcast.730, bf16[1,1,2,3,2,128,128]{6,5,2,4,3,1,0:T(8,128)(2,1)S(1)} %get-tuple-element.58, ...), kind=kLoop, calls=%fused_computation.26 | loop fusion | flops 4718592 | bytes 4718592 | tf_op jit(solution)/shard_map/concatenate | solution.py:17
  45.6 1.2 %copy.21 = bf16[1,2,3,2,128,128]{5,1,3,2,0,4:T(2,128)(2,1)} copy(bf16[1,2,3,2,128,128]{5,4,1,3,2,0:T(8,128)(2,1)S(1)} %pad_maximum_fusion.2) | data formatting | bytes 786432 | tf_op jit(solution)/shard_map/stack | solution.py:83
  46.7 3.8 %all-to-all-start.1 = ((bf16[1,2,3,2,128,128]{5,1,3,2,0,4:T(2,128)(2,1)}), bf16[1,2,3,2,128,128]{5,1,3,2,0,4:T(2,128)(2,1)S(1)}, u32[]{:S(2)}, u32[]{:S(2)}) async-start(bf16[1,2,3,2,128,128]{5,1,3,2,0,4:T(2,128)(2,1)} %copy.21), calls=%async_computation.1 | async-start | bytes 786432 | tf_op jit(solution)/shard_map/all_to_all | solution.py:159
  50.6 1.2 %fusion.199 = f32[16,12288]{1,0:T(8,128)} fusion(bf16[8,12288]{1,0:T(8,128)(2,1)S(1)} %reshape_squeeze.12), kind=kOutput, calls=%fused_computation.445 | convolution fusion | flops 3147648 | bytes 983040 | tf_op jit(solution)/shard_map/dot_general | solution.py:93
  51.8 1.2 %fusion.3 = f32[16,12288]{1,0:T(8,128)} fusion(f32[16,12288]{1,0:T(8,128)S(1)} %convolution_add_fusion.7, f32[16,12288]{1,0:T(8,128)S(1)} %copy-done.1, bf16[8,12288]{1,0:T(8,128)(2,1)S(1)} %reshape_squeeze.13), kind=kOutput, calls=%fused_computation.10 | convolution fusion | flops 3541248 | bytes 2555904 | tf_op jit(solution)/shard_map/dot_general | solution.py:93
  53.0 5.9 %all-to-all-done.1 = bf16[1,2,3,2,128,128]{5,1,3,2,0,4:T(2,128)(2,1)S(1)} async-done(((bf16[1,2,3,2,128,128]{5,1,3,2,0,4:T(2,128)(2,1)}), bf16[1,2,3,2,128,128]{5,1,3,2,0,4:T(2,128)(2,1)S(1)}, u32[]{:S(2)}, u32[]{:S(2)}) %all-to-all-start.1) | async-done | bytes 393248 | tf_op jit(solution)/shard_map/all_to_all | solution.py:159
  61.6 0.5 copy-done
  66.1 10.7 %all_to_all.54 = bf16[8,2,3,2,16,128]{5,4,2,1,3,0:T(8,128)(2,1)S(1)} all-to-all(bf16[8,2,3,2,16,128]{5,4,2,1,3,0:T(8,128)(2,1)S(1)} %pad_maximum_fusion.3), channel_id=1, replica_groups=mesh['energy'=8,'space'=4] {'energy'}, dimensions={0} | all-to-all | bytes 786432 | tf_op jit(solution)/shard_map/all_to_all | solution.py:165
  76.8 2.7 %collective-permute-start.2 = (bf16[1,1,3,2,128,128]{5,4,1,3,2,0:T(8,128)(2,1)S(1)}, bf16[1,1,3,2,128,128]{5,4,1,3,2,0:T(8,128)(2,1)S(1)}, u32[]{:S(2)}, u32[]{:S(2)}) collective-permute-start(bf16[1,1,3,2,128,128]{5,4,1,3,2,0:T(8,128)(2,1)S(1)} %get-tuple-element.51), channel_id=1, source_target_pairs={{0,1},{1,2},{2,3},{4,5},{5,6},{6,7},{8,9},{9,10},{10,11},{12,13},{... | collective-permute-start | bytes 589832 | tf_op jit(solution)/shard_map/ppermute | solution.py:15
  79.6 1.3 %collective-permute-start.3 = (bf16[1,1,3,2,128,128]{5,4,1,3,2,0:T(8,128)(2,1)S(1)}, bf16[1,1,3,2,128,128]{5,4,1,3,2,0:T(8,128)(2,1)S(1)}, u32[]{:S(2)}, u32[]{:S(2)}) collective-permute-start(bf16[1,1,3,2,128,128]{5,4,1,3,2,0:T(8,128)(2,1)S(1)} %get-tuple-element.52), channel_id=1, source_target_pairs={{1,0},{2,1},{3,2},{5,4},{6,5},{7,6},{9,8},{10,9},{11,10},{13,12},{... | collective-permute-start | bytes 589832 | tf_op jit(solution)/shard_map/ppermute | solution.py:16
  81.1 2.3 %collective-permute-done.2 = bf16[1,1,3,2,128,128]{5,4,1,3,2,0:T(8,128)(2,1)S(1)} collective-permute-done((bf16[1,1,3,2,128,128]{5,4,1,3,2,0:T(8,128)(2,1)S(1)}, bf16[1,1,3,2,128,128]{5,4,1,3,2,0:T(8,128)(2,1)S(1)}, u32[]{:S(2)}, u32[]{:S(2)}) %collective-permute-start.2) | collective-permute-done | bytes 196640 | tf_op jit(solution)/shard_map/ppermute | solution.py:15
  83.4 4.1 %collective-permute-done.3 = bf16[1,1,3,2,128,128]{5,4,1,3,2,0:T(8,128)(2,1)S(1)} collective-permute-done((bf16[1,1,3,2,128,128]{5,4,1,3,2,0:T(8,128)(2,1)S(1)}, bf16[1,1,3,2,128,128]{5,4,1,3,2,0:T(8,128)(2,1)S(1)}, u32[]{:S(2)}, u32[]{:S(2)}) %collective-permute-start.3) | collective-permute-done | bytes 196640 | tf_op jit(solution)/shard_map/ppermute | solution.py:16
  100.0 0.8 copy.26
  (211 shorter events, 33.5 us)
Async XLA Ops:
  2.6 13.5 %all-to-all-start = ((bf16[1,2,3,2,128,128]{5,1,3,2,0,4:T(2,128)(2,1)}), bf16[1,2,3,2,128,128]{5,1,3,2,0,4:T(2,128)(2,1)S(1)}, u32[]{:S(2)}, u32[]{:S(2)}) async-start(bf16[1,2,3,2,128,128]{5,1,3,2,0,4:T(2,128)(2,1)} %copy.19), calls=%async_computation | async-start | bytes 786432 | tf_op jit(solution)/shard_map/all_to_all | solution.py:160
  9.1 17.0 %collective-permute-start = (bf16[3,1,1,3,2,128,128]{6,5,2,4,3,1,0:T(8,128)(2,1)}, bf16[3,1,1,3,2,128,128]{6,5,2,4,3,1,0:T(8,128)(2,1)}, u32[]{:S(2)}, u32[]{:S(2)}) collective-permute-start(bf16[3,1,1,3,2,128,128]{6,5,2,4,3,1,0:T(8,128)(2,1)} %get-tuple-element.10), channel_id=1, source_target_pairs={{0,1},{1,2},{2,3},{4,5},{5,6},{6,7},{8,9},{9,10},{10,11},{12,13},{... | collective-permute-start | bytes 1769480 | tf_op jit(solution)/shard_map/ppermute | solution.py:15
  13.4 17.7 %collective-permute-start.1 = (bf16[3,1,1,3,2,128,128]{6,5,2,4,3,1,0:T(8,128)(2,1)}, bf16[3,1,1,3,2,128,128]{6,5,2,4,3,1,0:T(8,128)(2,1)}, u32[]{:S(2)}, u32[]{:S(2)}) collective-permute-start(bf16[3,1,1,3,2,128,128]{6,5,2,4,3,1,0:T(8,128)(2,1)} %get-tuple-element.11), channel_id=1, source_target_pairs={{1,0},{2,1},{3,2},{5,4},{6,5},{7,6},{9,8},{10,9},{11,10},{13,12},{... | collective-permute-start | bytes 1769480 | tf_op jit(solution)/shard_map/ppermute | solution.py:16
  45.4 6.3 %copy-start.1 = (f32[16,12288]{1,0:T(8,128)S(1)}, f32[16,12288]{1,0:T(8,128)}, u32[]{:S(2)}) copy-start(f32[16,12288]{1,0:T(8,128)} %fusion.203) | copy-start | bytes 2359300
  46.7 12.1 %all-to-all-start.1 = ((bf16[1,2,3,2,128,128]{5,1,3,2,0,4:T(2,128)(2,1)}), bf16[1,2,3,2,128,128]{5,1,3,2,0,4:T(2,128)(2,1)S(1)}, u32[]{:S(2)}, u32[]{:S(2)}) async-start(bf16[1,2,3,2,128,128]{5,1,3,2,0,4:T(2,128)(2,1)} %copy.21), calls=%async_computation.1 | async-start | bytes 786432 | tf_op jit(solution)/shard_map/all_to_all | solution.py:159
  61.0 1.1 %copy-start = (f32[16,12288]{1,0:T(8,128)S(1)}, f32[16,12288]{1,0:T(8,128)}, u32[]{:S(2)}) copy-start(f32[16,12288]{1,0:T(8,128)} %convolution_add_fusion.3) | copy-start | bytes 2359300
  61.0 1.4 %copy-start.2 = (f32[16,12288]{1,0:T(8,128)S(1)}, f32[16,12288]{1,0:T(8,128)}, u32[]{:S(2)}) copy-start(f32[16,12288]{1,0:T(8,128)} %fusion.199) | copy-start | bytes 2359300
  61.0 1.6 %copy-start.3 = (f32[16,12288]{1,0:T(8,128)S(1)}, f32[16,12288]{1,0:T(8,128)}, u32[]{:S(2)}) copy-start(f32[16,12288]{1,0:T(8,128)} %fusion.3) | copy-start | bytes 2359300
  76.8 6.5 %collective-permute-start.2 = (bf16[1,1,3,2,128,128]{5,4,1,3,2,0:T(8,128)(2,1)S(1)}, bf16[1,1,3,2,128,128]{5,4,1,3,2,0:T(8,128)(2,1)S(1)}, u32[]{:S(2)}, u32[]{:S(2)}) collective-permute-start(bf16[1,1,3,2,128,128]{5,4,1,3,2,0:T(8,128)(2,1)S(1)} %get-tuple-element.51), channel_id=1, source_target_pairs={{0,1},{1,2},{2,3},{4,5},{5,6},{6,7},{8,9},{9,10},{10,11},{12,13},{... | collective-permute-start | bytes 589832 | tf_op jit(solution)/shard_map/ppermute | solution.py:15
  79.6 8.0 %collective-permute-start.3 = (bf16[1,1,3,2,128,128]{5,4,1,3,2,0:T(8,128)(2,1)S(1)}, bf16[1,1,3,2,128,128]{5,4,1,3,2,0:T(8,128)(2,1)S(1)}, u32[]{:S(2)}, u32[]{:S(2)}) collective-permute-start(bf16[1,1,3,2,128,128]{5,4,1,3,2,0:T(8,128)(2,1)S(1)} %get-tuple-element.52), channel_id=1, source_target_pairs={{1,0},{2,1},{3,2},{5,4},{6,5},{7,6},{9,8},{10,9},{11,10},{13,12},{... | collective-permute-start | bytes 589832 | tf_op jit(solution)/shard_map/ppermute | solution.py:16
where the time goes:
time: 101 us
  matrix products  35.2 us (35%)
  waiting for transfers between devices  25.1 us (25%)
  starting transfers between devices  18.6 us (18%)
  blocking collectives  10.7 us (11%)
  local copies, waits for them, and re-layouts  6.76 us (7%)
  other arithmetic  3.78 us (4%)
    dot_general x144, matrix products, product(): return jnp.einsum(form, lhs, rhs, preferred_element_type=jnp.float32)  23.9 us
    dot_general x28, matrix products, plain_dot(): return jnp.dot(lhs, rhs, preferred_element_type=jnp.float32)  11.4 us
    all_to_all x1, blocking collectives, local(): lax.all_to_all(sigma_owned, 'energy', split_axis=0, concat_axis=4, tiled=...  10.7 us
    ppermute x2, waiting for transfers between devices, with_halo(): after = lax.ppermute(leading, axis, down)  9.03 us
    ppermute x2, waiting for transfers between devices, with_halo(): before = lax.ppermute(last, axis, up)  8.72 us
    ppermute x2, starting transfers between devices, with_halo(): before = lax.ppermute(last, axis, up)  6.99 us
    all_to_all x1, waiting for transfers between devices, local(): lax.all_to_all(screened, 'energy', split_axis=4, concat_axis=0, tiled=True)  5.9 us
    all_to_all x1, starting transfers between devices, local(): lax.all_to_all(propa_masked, 'energy', split_axis=4, concat_axis=0, tiled...  5.2 us
  transfers between devices with their start and end apart: 6, of which 6 were waited for; matrix products, arithmetic and copies ran while one was open for 7% of the time, Pallas kernels for 0%

commit v1 on v0

--- a/solution.py
+++ b/solution.py
@@ -3,6 +3,26 @@
 import jax.numpy as jnp
 from jax import lax
 from jax.sharding import PartitionSpec as P
+
+
+def scan_chunk_here(chunk, mesh_name):
+    step_out = lax.axis_size(mesh_name)
+    current_arr = lax.axis_index(mesh_name)
+    spare, x_now = (step_out, current_arr)
+    work_now = chunk.shape[4] // spare
+    current_value = jnp.roll(chunk, -x_now * work_now, 4)
+    t_next = lax.slice_in_dim(current_value, 0, work_now, axis=4)
+    shelf = [t_next]
+    p = 1
+    while p < spare:
+        row_out = lax.slice_in_dim(current_value, p * work_now, (p + 1) * work_now, axis=4)
+        reply = lax.ppermute(
+            row_out, mesh_name, [(dev_i, (dev_i + p) % spare) for dev_i in range(spare)]
+        )
+        shelf.append(reply)
+        p += 1
+    y_new = jnp.concatenate(shelf[::-1], 0)
+    return jnp.roll(y_new, (x_now + 1) * shelf[0].shape[0], 0)
 
 
 def with_halo(x, sides, width):
@@ -156,7 +176,7 @@
     propa_padded = rimmed[2]
     screened = sandwich(screen_padded, polar_padded).astype(jnp.bfloat16)
     screen_owned, propa_owned = (
-        lax.all_to_all(screened, "energy", split_axis=4, concat_axis=0, tiled=True),
+        scan_chunk_here(screened, mesh_name="energy"),
         lax.all_to_all(propa_masked, "energy", split_axis=4, concat_axis=0, tiled=True),
     )
     energy_count = screen_owned.shape[0]

time: 101 us -> 100 us (0.990)
  starting transfers between devices: 18.6 us -> 23 us
  waiting for transfers between devices: 25.1 us -> 21 us
    ppermute x0 -> x7, starting transfers between devices: none -> 6.35 us  [scan_chunk_here(): lax.ppermute(row_out, mesh_name, [(dev_i, (dev_i + p) % spare) for dev_i...]
    all_to_all x1 -> x0, waiting for transfers between devices: 5.9 us -> none  [local(): lax.all_to_all(screened, 'energy', split_axis=4, concat_axis=0, tiled=True)]
    ppermute x0 -> x7, waiting for transfers between devices: none -> 4.32 us  [scan_chunk_here(): lax.ppermute(row_out, mesh_name, [(dev_i, (dev_i + p) % spare) for dev_i...]
    all_to_all x1 -> x0, starting transfers between devices: 3.81 us -> none  [local(): lax.all_to_all(screened, 'energy', split_axis=4, concat_axis=0, tiled=True)]
    ppermute x2, waiting for transfers between devices: 9.03 us -> 7.05 us  [with_halo(): after = lax.ppermute(leading, axis, down)]
    ppermute x2, starting transfers between devices: 6.99 us -> 8.86 us  [with_halo(): before = lax.ppermute(last, axis, up)]
    another operation x2 -> x1, local copies, waits for them, and re-layouts: 1.93 us -> 0.77 us  [sandwich(): return jnp.stack(bands, axis=2)]
  transfers between devices with their start and end apart: 6 -> 12, of which waited for: 6 -> 9; matrix products, arithmetic and copies ran while one was open for 7% -> 6% of each run, Pallas kernels for 0% -> 0%
where the time goes in v1:
time: 100 us; the launch traced here: 99.7 us
  matrix products  34.4 us (34%)
  starting transfers between devices  23 us (23%)
  waiting for transfers between devices  21 us (21%)
  blocking collectives  10.8 us (11%)
  local copies, waits for them, and re-layouts  5.79 us (6%)
  other arithmetic  3.98 us (4%)
    dot_general x144, matrix products, product(): return jnp.einsum(form, lhs, rhs, preferred_element_type=jnp.float32)  23.9 us
    all_to_all x1, blocking collectives, local(): lax.all_to_all(sigma_owned, 'energy', split_axis=0, concat_axis=4, tiled=...  10.8 us
    dot_general x28, matrix products, plain_dot(): return jnp.dot(lhs, rhs, preferred_element_type=jnp.float32)  10.5 us
    ppermute x2, starting transfers between devices, with_halo(): before = lax.ppermute(last, axis, up)  8.86 us
    ppermute x2, waiting for transfers between devices, with_halo(): before = lax.ppermute(last, axis, up)  8.19 us
    ppermute x2, waiting for transfers between devices, with_halo(): after = lax.ppermute(leading, axis, down)  7.05 us
    ppermute x7, starting transfers between devices, scan_chunk_here(): lax.ppermute(row_out, mesh_name, [(dev_i, (dev_i + p) % spare) for dev_i...  6.35 us
    all_to_all x1, starting transfers between devices, local(): lax.all_to_all(propa_masked, 'energy', split_axis=4, concat_axis=0, tiled...  5.2 us
  transfers between devices with their start and end apart: 12, of which 9 were waited for; matrix products, arithmetic and copies ran while one was open for 6% of the time, Pallas kernels for 0%

profile of v1, /device:TPU:0, one launch (start us, length us, event | category | flops | bytes accessed | tf_op | source)
XLA Modules:
  0.0 99.7 jit_solution(11622258553412747567)
XLA Ops:
  0.1 1.4 %fusion.88 = (bf16[1,1,2,3,2,128,128]{6,5,2,4,3,1,0:T(8,128)(2,1)S(1)}, bf16[1,1,2,3,2,128,128]{6,5,2,4,3,1,0:T(8,128)(2,1)S(1)}, bf16[1,2,3,2,128,128]{5,4,1,3,2,0:T(8,128)(2,1)S(1)}) fusion(bf16[1,2,3,2,128,128]{5,4,3,2,1,0:T(8,128)(2,1)} %param.3, bf16[2,3]{0,1:T(4,128)(2,1)S(1)} %select_convert_fusion, bf16[1,2,3,2,128,128]{5,4,3,2,1,0:T(8,128)(2,1)} %param.4, ...), kind=kLoop, calls=%fused_computation.197 | loop fusion | flops 589824 | bytes 2359308 | tf_op jit(solution)/shard_map/stack | solution.py:173
  1.5 1.2 %copy.20 = bf16[1,2,3,2,128,128]{5,1,3,2,0,4:T(2,128)(2,1)} copy(bf16[1,2,3,2,128,128]{5,4,1,3,2,0:T(8,128)(2,1)S(1)} %get-tuple-element.66) | data formatting | bytes 786432 | tf_op jit(solution)/shard_map/mul | solution.py:49
  2.6 5.2 %all-to-all-start = ((bf16[1,2,3,2,128,128]{5,1,3,2,0,4:T(2,128)(2,1)}), bf16[1,2,3,2,128,128]{5,1,3,2,0,4:T(2,128)(2,1)S(1)}, u32[]{:S(2)}, u32[]{:S(2)}) async-start(bf16[1,2,3,2,128,128]{5,1,3,2,0,4:T(2,128)(2,1)} %copy.20), calls=%async_computation | async-start | bytes 786432 | tf_op jit(solution)/shard_map/all_to_all | solution.py:180
  8.0 1.2 %fusion.363 = (bf16[3,1,1,3,2,128,128]{6,5,2,4,3,1,0:T(8,128)(2,1)}, bf16[3,1,1,3,2,128,128]{6,5,2,4,3,1,0:T(8,128)(2,1)}) fusion(bf16[3,1,2,3,2,128,128]{6,5,2,4,3,1,0:T(8,128)(2,1)S(1)} %pad_maximum_fusion.1), kind=kLoop, calls=%fused_computation.620 | loop fusion | bytes 2359296 | tf_op jit(solution)/shard_map/slice | solution.py:33
  9.1 4.3 %collective-permute-start = (bf16[3,1,1,3,2,128,128]{6,5,2,4,3,1,0:T(8,128)(2,1)}, bf16[3,1,1,3,2,128,128]{6,5,2,4,3,1,0:T(8,128)(2,1)}, u32[]{:S(2)}, u32[]{:S(2)}) collective-permute-start(bf16[3,1,1,3,2,128,128]{6,5,2,4,3,1,0:T(8,128)(2,1)} %get-tuple-element.10), channel_id=1, source_target_pairs={{0,1},{1,2},{2,3},{4,5},{5,6},{6,7},{8,9},{9,10},{10,11},{12,13},{... | collective-permute-start | bytes 1769480 | tf_op jit(solution)/shard_map/ppermute | solution.py:35
  13.4 1.3 %collective-permute-start.1 = (bf16[3,1,1,3,2,128,128]{6,5,2,4,3,1,0:T(8,128)(2,1)}, bf16[3,1,1,3,2,128,128]{6,5,2,4,3,1,0:T(8,128)(2,1)}, u32[]{:S(2)}, u32[]{:S(2)}) collective-permute-start(bf16[3,1,1,3,2,128,128]{6,5,2,4,3,1,0:T(8,128)(2,1)} %get-tuple-element.11), channel_id=1, source_target_pairs={{1,0},{2,1},{3,2},{5,4},{6,5},{7,6},{9,8},{10,9},{11,10},{13,12},{... | collective-permute-start | bytes 1769480 | tf_op jit(solution)/shard_map/ppermute | solution.py:36
  14.7 1.4 %all-to-all-done = bf16[1,2,3,2,128,128]{5,1,3,2,0,4:T(2,128)(2,1)S(1)} async-done(((bf16[1,2,3,2,128,128]{5,1,3,2,0,4:T(2,128)(2,1)}), bf16[1,2,3,2,128,128]{5,1,3,2,0,4:T(2,128)(2,1)S(1)}, u32[]{:S(2)}, u32[]{:S(2)}) %all-to-all-start) | async-done | bytes 393248 | tf_op jit(solution)/shard_map/all_to_all | solution.py:180
  17.9 1.2 %fusion.3 = f32[16,12288]{1,0:T(8,128)} fusion(f32[16,12288]{1,0:T(8,128)S(1)} %convolution_add_fusion.7, f32[16,12288]{1,0:T(8,128)S(1)} %fusion.208, bf16[8,12288]{1,0:T(8,128)(2,1)S(1)} %reshape_squeeze.13), kind=kOutput, calls=%fused_computation.10 | convolution fusion | flops 3541248 | bytes 2555904 | tf_op jit(solution)/shard_map/dot_general | solution.py:113
  19.1 7.0 %collective-permute-done = bf16[3,1,1,3,2,128,128]{6,5,2,4,3,1,0:T(8,128)(2,1)} collective-permute-done((bf16[3,1,1,3,2,128,128]{6,5,2,4,3,1,0:T(8,128)(2,1)}, bf16[3,1,1,3,2,128,128]{6,5,2,4,3,1,0:T(8,128)(2,1)}, u32[]{:S(2)}, u32[]{:S(2)}) %collective-permute-start) | collective-permute-done | bytes 589856 | tf_op jit(solution)/shard_map/ppermute | solution.py:35
  26.2 4.9 %collective-permute-done.1 = bf16[3,1,1,3,2,128,128]{6,5,2,4,3,1,0:T(8,128)(2,1)} collective-permute-done((bf16[3,1,1,3,2,128,128]{6,5,2,4,3,1,0:T(8,128)(2,1)}, bf16[3,1,1,3,2,128,128]{6,5,2,4,3,1,0:T(8,128)(2,1)}, u32[]{:S(2)}, u32[]{:S(2)}) %collective-permute-start.1) | collective-permute-done | bytes 589856 | tf_op jit(solution)/shard_map/ppermute | solution.py:36
  31.1 1.4 %pad_maximum_fusion = bf16[3,1,4,3,2,128,128]{6,5,2,4,3,1,0:T(8,128)(2,1)S(1)} fusion(bf16[3,1,1,3,2,128,128]{6,5,2,4,3,1,0:T(8,128)(2,1)} %collective-permute-done.1, bf16[1,1,2,3,2,128,128]{6,5,2,4,3,1,0:T(8,128)(2,1)S(1)} %bitcast.724, bf16[1,1,2,3,2,128,128]{6,5,2,4,3,1,0:T(8,128)(2,1)S(1)} %get-tuple-element.65, ...), kind=kLoop, calls=%fused_computation.26 | loop fusion | flops 4718592 | bytes 4718592 | tf_op jit(solution)/shard_map/concatenate | solution.py:37
  45.8 1.2 %collective-permute-start.2 = (bf16[1,2,3,2,16,128]{5,4,1,3,2,0:T(8,128)(2,1)S(1)}, bf16[1,2,3,2,16,128]{5,4,1,3,2,0:T(8,128)(2,1)S(1)}, u32[]{:S(2)}, u32[]{:S(2)}) collective-permute-start(bf16[1,2,3,2,16,128]{5,4,1,3,2,0:T(8,128)(2,1)S(1)} %get-tuple-element.61), channel_id=1, source_target_pairs={{0,28},{4,0},{8,4},{12,8},{16,12},{20,16},{24,20},{28,24},{1,29},{... | collective-permute-start | bytes 147464 | tf_op jit(solution)/shard_map/ppermute | solution.py:19
  47.0 1.2 %fusion.204 = f32[16,12288]{1,0:T(8,128)} fusion(bf16[8,12288]{1,0:T(8,128)(2,1)S(1)} %reshape_squeeze.12), kind=kOutput, calls=%fused_computation.470 | convolution fusion | flops 3147648 | bytes 983040 | tf_op jit(solution)/shard_map/dot_general | solution.py:113
  48.2 1.4 %collective-permute-start.3 = (bf16[1,2,3,2,16,128]{5,4,1,3,2,0:T(8,128)(2,1)S(1)}, bf16[1,2,3,2,16,128]{5,4,1,3,2,0:T(8,128)(2,1)S(1)}, u32[]{:S(2)}, u32[]{:S(2)}) collective-permute-start(bf16[1,2,3,2,16,128]{5,4,1,3,2,0:T(8,128)(2,1)S(1)} %get-tuple-element.60), channel_id=1, source_target_pairs={{0,24},{4,28},{8,0},{12,4},{16,8},{20,12},{24,16},{28,20},{1,25},{... | collective-permute-start | bytes 147464 | tf_op jit(solution)/shard_map/ppermute | solution.py:19
  50.0 1.5 %collective-permute-start.5 = (bf16[1,2,3,2,16,128]{5,4,1,3,2,0:T(8,128)(2,1)S(1)}, bf16[1,2,3,2,16,128]{5,4,1,3,2,0:T(8,128)(2,1)S(1)}, u32[]{:S(2)}, u32[]{:S(2)}) collective-permute-start(bf16[1,2,3,2,16,128]{5,4,1,3,2,0:T(8,128)(2,1)S(1)} %get-tuple-element.58), channel_id=1, source_target_pairs={{0,16},{4,20},{8,24},{12,28},{16,0},{20,4},{24,8},{28,12},{1,17},{... | collective-permute-start | bytes 147464 | tf_op jit(solution)/shard_map/ppermute | solution.py:19
  51.7 1.5 %collective-permute-start.7 = (bf16[1,2,3,2,16,128]{5,4,1,3,2,0:T(8,128)(2,1)S(1)}, bf16[1,2,3,2,16,128]{5,4,1,3,2,0:T(8,128)(2,1)S(1)}, u32[]{:S(2)}, u32[]{:S(2)}) collective-permute-start(bf16[1,2,3,2,16,128]{5,4,1,3,2,0:T(8,128)(2,1)S(1)} %get-tuple-element.56), channel_id=1, source_target_pairs={{0,8},{4,12},{8,16},{12,20},{16,24},{20,28},{24,0},{28,4},{1,9},{5... | collective-permute-start | bytes 147464 | tf_op jit(solution)/shard_map/ppermute | solution.py:19
  53.5 1.1 %collective-permute-done.5 = bf16[1,2,3,2,16,128]{5,4,1,3,2,0:T(8,128)(2,1)S(1)} collective-permute-done((bf16[1,2,3,2,16,128]{5,4,1,3,2,0:T(8,128)(2,1)S(1)}, bf16[1,2,3,2,16,128]{5,4,1,3,2,0:T(8,128)(2,1)S(1)}, u32[]{:S(2)}, u32[]{:S(2)}) %collective-permute-start.5) | collective-permute-done | bytes 49184 | tf_op jit(solution)/shard_map/ppermute | solution.py:19
  55.1 2.1 %collective-permute-done.7 = bf16[1,2,3,2,16,128]{5,4,1,3,2,0:T(8,128)(2,1)S(1)} collective-permute-done((bf16[1,2,3,2,16,128]{5,4,1,3,2,0:T(8,128)(2,1)S(1)}, bf16[1,2,3,2,16,128]{5,4,1,3,2,0:T(8,128)(2,1)S(1)}, u32[]{:S(2)}, u32[]{:S(2)}) %collective-permute-start.7) | collective-permute-done | bytes 49184 | tf_op jit(solution)/shard_map/ppermute | solution.py:19
  58.2 1.2 %fusion.206 = f32[16,12288]{1,0:T(8,128)} fusion(bf16[8,12288]{1,0:T(8,128)(2,1)S(1)} %reshape_squeeze.15), kind=kOutput, calls=%fused_computation.471 | convolution fusion | flops 3147648 | bytes 983040 | tf_op jit(solution)/shard_map/dot_general | solution.py:113
  66.1 10.8 %all_to_all.36 = bf16[8,2,3,2,16,128]{5,4,2,1,3,0:T(8,128)(2,1)S(1)} all-to-all(bf16[8,2,3,2,16,128]{5,4,2,1,3,0:T(8,128)(2,1)S(1)} %pad_maximum_fusion.2), channel_id=1, replica_groups=mesh['energy'=8,'space'=4] {'energy'}, dimensions={0} | all-to-all | bytes 786432 | tf_op jit(solution)/shard_map/all_to_all | solution.py:185
  77.0 1.3 %collective-permute-start.10 = (bf16[1,1,3,2,128,128]{5,4,1,3,2,0:T(8,128)(2,1)S(1)}, bf16[1,1,3,2,128,128]{5,4,1,3,2,0:T(8,128)(2,1)S(1)}, u32[]{:S(2)}, u32[]{:S(2)}) collective-permute-start(bf16[1,1,3,2,128,128]{5,4,1,3,2,0:T(8,128)(2,1)S(1)} %get-tuple-element.54), channel_id=1, source_target_pairs={{1,0},{2,1},{3,2},{5,4},{6,5},{7,6},{9,8},{10,9},{11,10},{13,12},{... | collective-permute-start | bytes 589832 | tf_op jit(solution)/shard_map/ppermute | solution.py:36
  78.3 4.6 %collective-permute-start.9 = (bf16[1,1,3,2,128,128]{5,4,1,3,2,0:T(8,128)(2,1)S(1)}, bf16[1,1,3,2,128,128]{5,4,1,3,2,0:T(8,128)(2,1)S(1)}, u32[]{:S(2)}, u32[]{:S(2)}) collective-permute-start(bf16[1,1,3,2,128,128]{5,4,1,3,2,0:T(8,128)(2,1)S(1)} %get-tuple-element.53), channel_id=1, source_target_pairs={{0,1},{1,2},{2,3},{4,5},{5,6},{6,7},{8,9},{9,10},{10,11},{12,13},{... | collective-permute-start | bytes 589832 | tf_op jit(solution)/shard_map/ppermute | solution.py:35
  83.1 2.1 %collective-permute-done.10 = bf16[1,1,3,2,128,128]{5,4,1,3,2,0:T(8,128)(2,1)S(1)} collective-permute-done((bf16[1,1,3,2,128,128]{5,4,1,3,2,0:T(8,128)(2,1)S(1)}, bf16[1,1,3,2,128,128]{5,4,1,3,2,0:T(8,128)(2,1)S(1)}, u32[]{:S(2)}, u32[]{:S(2)}) %collective-permute-start.10) | collective-permute-done | bytes 196640 | tf_op jit(solution)/shard_map/ppermute | solution.py:36
  85.2 1.2 %collective-permute-done.9 = bf16[1,1,3,2,128,128]{5,4,1,3,2,0:T(8,128)(2,1)S(1)} collective-permute-done((bf16[1,1,3,2,128,128]{5,4,1,3,2,0:T(8,128)(2,1)S(1)}, bf16[1,1,3,2,128,128]{5,4,1,3,2,0:T(8,128)(2,1)S(1)}, u32[]{:S(2)}, u32[]{:S(2)}) %collective-permute-start.9) | collective-permute-done | bytes 196640 | tf_op jit(solution)/shard_map/ppermute | solution.py:35
  (238 shorter events, 37.3 us)
Async XLA Ops:
  2.6 13.5 %all-to-all-start = ((bf16[1,2,3,2,128,128]{5,1,3,2,0,4:T(2,128)(2,1)}), bf16[1,2,3,2,128,128]{5,1,3,2,0,4:T(2,128)(2,1)S(1)}, u32[]{:S(2)}, u32[]{:S(2)}) async-start(bf16[1,2,3,2,128,128]{5,1,3,2,0,4:T(2,128)(2,1)} %copy.20), calls=%async_computation | async-start | bytes 786432 | tf_op jit(solution)/shard_map/all_to_all | solution.py:180
  9.1 17.0 %collective-permute-start = (bf16[3,1,1,3,2,128,128]{6,5,2,4,3,1,0:T(8,128)(2,1)}, bf16[3,1,1,3,2,128,128]{6,5,2,4,3,1,0:T(8,128)(2,1)}, u32[]{:S(2)}, u32[]{:S(2)}) collective-permute-start(bf16[3,1,1,3,2,128,128]{6,5,2,4,3,1,0:T(8,128)(2,1)} %get-tuple-element.10), channel_id=1, source_target_pairs={{0,1},{1,2},{2,3},{4,5},{5,6},{6,7},{8,9},{9,10},{10,11},{12,13},{... | collective-permute-start | bytes 1769480 | tf_op jit(solution)/shard_map/ppermute | solution.py:35
  13.4 17.7 %collective-permute-start.1 = (bf16[3,1,1,3,2,128,128]{6,5,2,4,3,1,0:T(8,128)(2,1)}, bf16[3,1,1,3,2,128,128]{6,5,2,4,3,1,0:T(8,128)(2,1)}, u32[]{:S(2)}, u32[]{:S(2)}) collective-permute-start(bf16[3,1,1,3,2,128,128]{6,5,2,4,3,1,0:T(8,128)(2,1)} %get-tuple-element.11), channel_id=1, source_target_pairs={{1,0},{2,1},{3,2},{5,4},{6,5},{7,6},{9,8},{10,9},{11,10},{13,12},{... | collective-permute-start | bytes 1769480 | tf_op jit(solution)/shard_map/ppermute | solution.py:36
  45.8 5.9 %collective-permute-start.2 = (bf16[1,2,3,2,16,128]{5,4,1,3,2,0:T(8,128)(2,1)S(1)}, bf16[1,2,3,2,16,128]{5,4,1,3,2,0:T(8,128)(2,1)S(1)}, u32[]{:S(2)}, u32[]{:S(2)}) collective-permute-start(bf16[1,2,3,2,16,128]{5,4,1,3,2,0:T(8,128)(2,1)S(1)} %get-tuple-element.61), channel_id=1, source_target_pairs={{0,28},{4,0},{8,4},{12,8},{16,12},{20,16},{24,20},{28,24},{1,29},{... | collective-permute-start | bytes 147464 | tf_op jit(solution)/shard_map/ppermute | solution.py:19
  48.2 5.0 %collective-permute-start.3 = (bf16[1,2,3,2,16,128]{5,4,1,3,2,0:T(8,128)(2,1)S(1)}, bf16[1,2,3,2,16,128]{5,4,1,3,2,0:T(8,128)(2,1)S(1)}, u32[]{:S(2)}, u32[]{:S(2)}) collective-permute-start(bf16[1,2,3,2,16,128]{5,4,1,3,2,0:T(8,128)(2,1)S(1)} %get-tuple-element.60), channel_id=1, source_target_pairs={{0,24},{4,28},{8,0},{12,4},{16,8},{20,12},{24,16},{28,20},{1,25},{... | collective-permute-start | bytes 147464 | tf_op jit(solution)/shard_map/ppermute | solution.py:19
  49.7 3.8 %collective-permute-start.4 = (bf16[1,2,3,2,16,128]{5,4,1,3,2,0:T(8,128)(2,1)S(1)}, bf16[1,2,3,2,16,128]{5,4,1,3,2,0:T(8,128)(2,1)S(1)}, u32[]{:S(2)}, u32[]{:S(2)}) collective-permute-start(bf16[1,2,3,2,16,128]{5,4,1,3,2,0:T(8,128)(2,1)S(1)} %get-tuple-element.59), channel_id=1, source_target_pairs={{0,20},{4,24},{8,28},{12,0},{16,4},{20,8},{24,12},{28,16},{1,21},{... | collective-permute-start | bytes 147464 | tf_op jit(solution)/shard_map/ppermute | solution.py:19
  50.0 4.5 %collective-permute-start.5 = (bf16[1,2,3,2,16,128]{5,4,1,3,2,0:T(8,128)(2,1)S(1)}, bf16[1,2,3,2,16,128]{5,4,1,3,2,0:T(8,128)(2,1)S(1)}, u32[]{:S(2)}, u32[]{:S(2)}) collective-permute-start(bf16[1,2,3,2,16,128]{5,4,1,3,2,0:T(8,128)(2,1)S(1)} %get-tuple-element.58), channel_id=1, source_target_pairs={{0,16},{4,20},{8,24},{12,28},{16,0},{20,4},{24,8},{28,12},{1,17},{... | collective-permute-start | bytes 147464 | tf_op jit(solution)/shard_map/ppermute | solution.py:19
  51.5 3.6 %collective-permute-start.6 = (bf16[1,2,3,2,16,128]{5,4,1,3,2,0:T(8,128)(2,1)S(1)}, bf16[1,2,3,2,16,128]{5,4,1,3,2,0:T(8,128)(2,1)S(1)}, u32[]{:S(2)}, u32[]{:S(2)}) collective-permute-start(bf16[1,2,3,2,16,128]{5,4,1,3,2,0:T(8,128)(2,1)S(1)} %get-tuple-element.57), channel_id=1, source_target_pairs={{0,12},{4,16},{8,20},{12,24},{16,28},{20,0},{24,4},{28,8},{1,13},{... | collective-permute-start | bytes 147464 | tf_op jit(solution)/shard_map/ppermute | solution.py:19
  51.7 5.5 %collective-permute-start.7 = (bf16[1,2,3,2,16,128]{5,4,1,3,2,0:T(8,128)(2,1)S(1)}, bf16[1,2,3,2,16,128]{5,4,1,3,2,0:T(8,128)(2,1)S(1)}, u32[]{:S(2)}, u32[]{:S(2)}) collective-permute-start(bf16[1,2,3,2,16,128]{5,4,1,3,2,0:T(8,128)(2,1)S(1)} %get-tuple-element.56), channel_id=1, source_target_pairs={{0,8},{4,12},{8,16},{12,20},{16,24},{20,28},{24,0},{28,4},{1,9},{5... | collective-permute-start | bytes 147464 | tf_op jit(solution)/shard_map/ppermute | solution.py:19
  53.2 4.6 %collective-permute-start.8 = (bf16[1,2,3,2,16,128]{5,4,1,3,2,0:T(8,128)(2,1)S(1)}, bf16[1,2,3,2,16,128]{5,4,1,3,2,0:T(8,128)(2,1)S(1)}, u32[]{:S(2)}, u32[]{:S(2)}) collective-permute-start(bf16[1,2,3,2,16,128]{5,4,1,3,2,0:T(8,128)(2,1)S(1)} %get-tuple-element.55), channel_id=1, source_target_pairs={{0,4},{4,8},{8,12},{12,16},{16,20},{20,24},{24,28},{28,0},{1,5},{5... | collective-permute-start | bytes 147464 | tf_op jit(solution)/shard_map/ppermute | solution.py:19
  60.1 1.1 %copy-start = (f32[16,12288]{1,0:T(8,128)S(1)}, f32[16,12288]{1,0:T(8,128)}, u32[]{:S(2)}) copy-start(f32[16,12288]{1,0:T(8,128)} %fusion.206) | copy-start | bytes 2359300
  61.2 1.1 %copy-start.1 = (f32[16,12288]{1,0:T(8,128)S(1)}, f32[16,12288]{1,0:T(8,128)}, u32[]{:S(2)}) copy-start(f32[16,12288]{1,0:T(8,128)} %fusion.3) | copy-start | bytes 2359300
  61.2 1.4 %copy-start.2 = (f32[16,12288]{1,0:T(8,128)S(1)}, f32[16,12288]{1,0:T(8,128)}, u32[]{:S(2)}) copy-start(f32[16,12288]{1,0:T(8,128)} %fusion.204) | copy-start | bytes 2359300
  77.0 8.2 %collective-permute-start.10 = (bf16[1,1,3,2,128,128]{5,4,1,3,2,0:T(8,128)(2,1)S(1)}, bf16[1,1,3,2,128,128]{5,4,1,3,2,0:T(8,128)(2,1)S(1)}, u32[]{:S(2)}, u32[]{:S(2)}) collective-permute-start(bf16[1,1,3,2,128,128]{5,4,1,3,2,0:T(8,128)(2,1)S(1)} %get-tuple-element.54), channel_id=1, source_target_pairs={{1,0},{2,1},{3,2},{5,4},{6,5},{7,6},{9,8},{10,9},{11,10},{13,12},{... | collective-permute-start | bytes 589832 | tf_op jit(solution)/shard_map/ppermute | solution.py:36
  78.3 8.1 %collective-permute-start.9 = (bf16[1,1,3,2,128,128]{5,4,1,3,2,0:T(8,128)(2,1)S(1)}, bf16[1,1,3,2,128,128]{5,4,1,3,2,0:T(8,128)(2,1)S(1)}, u32[]{:S(2)}, u32[]{:S(2)}) collective-permute-start(bf16[1,1,3,2,128,128]{5,4,1,3,2,0:T(8,128)(2,1)S(1)} %get-tuple-element.53), channel_id=1, source_target_pairs={{0,1},{1,2},{2,3},{4,5},{5,6},{6,7},{8,9},{9,10},{10,11},{12,13},{... | collective-permute-start | bytes 589832 | tf_op jit(solution)/shard_map/ppermute | solution.py:35
